TPU v7x, 128 devices: a whole 4x4x4 slice. The times are simulated.
128 devices in a mesh: orb: 8 (over x, y_lo), aux: 16 (over z, y_hi, core).
Axes of the slice: x: 4, y: 4 (y_hi: 2, y_lo: 2; y = y_hi * 2 + y_lo), z: 4, core: 2. Of those that a mesh axis runs over, the one named last changes fastest.
Arguments:
- raw_rows: bfloat16 [512, 2048, 128], P('orb', 'aux'), may hold values from -4 to 4
- fit_metric: bfloat16 [512, 512, 512], P(('orb', 'aux'))
- domain: int32 [512, 512], P('orb'), may hold values from 0 to 127, as said below
- counts: int32 [512, 16], P('orb'), may hold values from 16 to 64, as said below
- orbital_ids: int32 [512], P(('orb', 'aux')), may hold values from 0 to 511, each once
- occ_energy: float32 [512], replicated, may hold values from -1.5 to -0.3
- osv_energy: bfloat16 [512, 128], P(('orb', 'aux')), may hold values from 0.29882812 to 3
- matchings: int32 [4, 8], replicated, may hold values from 0 to 7, as said below
- screening: int32 [512, 5, 4], P(('orb', 'aux')), may hold values 0 or 1
Outputs:
- density: float32 [512, 2048, 128], P('orb', 'aux')
- pair_energy: float32 [512, 5, 4], P(('orb', 'aux'))
Inputs may be any that keep to these rules, and one draw needn't show every extreme that they name: `counts`: every row sums to 512; every entry is at most 64, and every row has an entry equal to 64. `domain`: the positions of a row are taken by owner 0 first, then owner 1 and so on, in the numbers that counts gives; within one owner's run the entries are distinct. `matchings`: row q maps orb index o to o XOR m_q, with a mask m_q from 1 to 7; rounds may repeat a mask.
All inputs are finite; a program needn't handle non-finite values. No bound on the sum of `screening` on one device may be relied on, other than what follows from the above.
Results may differ from a plain program's by a relative error of at most 0.0029.
Values may be sent and summed in bfloat16 or wider, within the bound.
No kernel may reach another device: no remote copies, remote signals or barrier semaphores. Data moves between devices by JAX's collectives and lax.ppermute only.
A program may use at most 128 MiB of HBM per device.

v0:
```python
import functools

import jax
import jax.numpy as jnp
from jax import lax
from jax.experimental import pallas as pl
from jax.experimental.pallas import tpu as pltpu
from jax.sharding import PartitionSpec as P

PAIR_SCALE = 1.3
BF16 = jnp.bfloat16
F32 = jnp.float32
I32 = jnp.int32
NOSV = 128
NFIT = 512
OCC = 4
AUXD = 128
NAUX_DEV = 16
NAUX = AUXD * NAUX_DEV
CAP = 64
CHUNKS = NFIT // CAP
TAIL = 32
ROWS = NFIT + TAIL
TILE = 512
PARTS = 4
SLAB = OCC * NOSV
VMEM_LIMIT = 28 * 1024 * 1024


def params(**kw):
    return pltpu.CompilerParams(vmem_limit_bytes=VMEM_LIMIT, **kw)


def pack_kernel(
    where_am_i, domain_in, counts_in, raw, out, domain, counts, rows, packed, columns, in_sems, out_sems, sems
):
    group = raw.shape[0]
    part = group // PARTS

    def load(i):
        span = pl.ds(i * part, part)
        return pltpu.make_async_copy(raw.at[span], rows.at[span], in_sems.at[i])

    def save(i):
        span = pl.ds(i * part, part)
        return pltpu.make_async_copy(packed.at[span], out.at[span], out_sems.at[i])

    small = (
        pltpu.make_async_copy(counts_in, counts, sems.at[0]),
        pltpu.make_async_copy(domain_in, domain, sems.at[1]),
    )
    for copy in small:
        copy.start()
    for i in range(PARTS):
        load(i).start()
    for copy in small:
        copy.wait()
    me = where_am_i[0]
    owner = lax.broadcasted_iota(I32, (NAUX_DEV, group), 0)
    start = jnp.sum(jnp.where(owner < me, counts[...], 0), axis=0, keepdims=True)
    size = jnp.sum(jnp.where(owner == me, counts[...], 0), axis=0, keepdims=True)
    both = jnp.concatenate([start] * 4 + [start + size] * 4, axis=0).astype(F32).T.astype(I32)
    start = both[:, 0:1]
    end = both[:, 4:5]
    lane = lax.broadcasted_iota(I32, (group, NOSV), 1)
    code = jnp.zeros((group, NOSV), I32)
    for i in range(4):
        position = lane + i * NOSV
        inside = (position >= start) & (position < end)
        code += jnp.where(inside, domain[:, i * NOSV : (i + 1) * NOSV] + 1, 0)
    code = (code + pltpu.roll(code, CAP, 1) - 1).astype(F32)
    columns[...] = code.T

    lanes = lax.broadcasted_iota(I32, (CAP, AUXD), 1).astype(F32)
    for i in range(PARTS):
        load(i).wait()
        for g in range(i * part, (i + 1) * part):
            pick = jnp.where(lanes == columns[:CAP, g : g + 1], 1.0, 0.0).astype(BF16)
            packed[g] = jnp.dot(pick, rows[g], preferred_element_type=F32).astype(BF16)
        save(i).start()
    for i in range(PARTS):
        save(i).wait()


def pack_rows(where_am_i, domain, counts, raw_rows):
    group = raw_rows.shape[0]
    smem = pl.BlockSpec(memory_space=pltpu.SMEM)
    hbm = pl.BlockSpec(memory_space=pltpu.HBM)
    return pl.pallas_call(
        pack_kernel,
        in_specs=[smem, hbm, hbm, hbm],
        out_specs=hbm,
        out_shape=pltpu.HBM((group, CAP, NOSV), BF16),
        scratch_shapes=[
            pltpu.VMEM(domain.shape, I32),
            pltpu.VMEM(counts.shape, I32),
            pltpu.VMEM(raw_rows.shape, BF16),
            pltpu.VMEM((group, CAP, NOSV), BF16),
            pltpu.VMEM((NOSV, group), F32),
            pltpu.SemaphoreType.DMA((PARTS,)),
            pltpu.SemaphoreType.DMA((PARTS,)),
            pltpu.SemaphoreType.DMA((2,)),
        ],
        compiler_params=params(),
        name="pack_rows",
    )(where_am_i, *(pltpu.with_memory_space_constraint(x, pltpu.HBM) for x in (domain, counts, raw_rows)))


def tables_kernel(where_am_i, counts, ids, occ, domain, osv, out, windows, table):
    me = where_am_i[0]
    lane = lax.broadcasted_iota(I32, (1, NOSV), 1)
    energies = osv[...].astype(F32)
    for k in range(OCC):
        row = domain[pl.ds(me * OCC + k, 1), :]
        for i in range(4):
            windows[2 * i : 2 * i + 1, :] = row[:, i * NOSV : (i + 1) * NOSV]
            if i < 3:
                windows[2 * i + 1 : 2 * i + 2, :] = row[:, i * NOSV + CAP : (i + 1) * NOSV + CAP]
        table[...] = jnp.zeros(table.shape, F32)
        starts = jnp.zeros((1, NOSV), I32)
        start = jnp.int32(0)
        for a in range(NAUX_DEV):
            end = start + counts[a, me * OCC + k]
            chunk = jnp.minimum(start // CAP, CHUNKS - 2)
            at = chunk * CAP
            entry = windows[pl.ds(chunk, 1), :]
            entry = jnp.where((lane >= start - at) & (lane < end - at), entry, -1)
            table[a : a + 1, :] = entry.astype(F32)
            starts = jnp.where(lane == a, at, starts)
            start = end
        table[16:17, :] = starts.astype(F32)
        term = energies[k : k + 1, :] - occ[ids[k]]
        for i in range(3):
            rounded = term.astype(BF16).astype(F32)
            table[17 + i : 18 + i, :] = rounded
            term = term - rounded
        out[k] = table[...].astype(BF16)


def slot_tables(where_am_i, counts, ids, occ, domain, osv):
    smem = pl.BlockSpec(memory_space=pltpu.SMEM)
    vmem = pl.BlockSpec(memory_space=pltpu.VMEM)
    return pl.pallas_call(
        tables_kernel,
        in_specs=[smem, smem, smem, smem, vmem, vmem],
        out_specs=vmem,
        out_shape=jax.ShapeDtypeStruct((OCC, TAIL, NOSV), BF16),
        scratch_shapes=[pltpu.VMEM((8, NOSV), I32), pltpu.VMEM((TAIL, NOSV), F32)],
        compiler_params=params(),
        name="slot_tables",
    )(where_am_i, counts, ids, occ, domain, osv)


def fit_kernel(where_am_i, counts, received, metric, tail, fitted, block, acc, whole, sems):
    sub = lax.broadcasted_iota(I32, (CAP, NOSV), 0)
    starts = [jnp.int32(0)] * OCC
    for a in range(NAUX_DEV):
        for k in range(OCC):
            at = pl.multiple_of(jnp.minimum(starts[k] // CAP, CHUNKS - 1) * CAP, CAP)
            here = sub >= starts[k] % CAP
            rows = received[a, k].astype(F32)
            pltpu.store(acc.at[k, pl.ds(at, CAP), :], rows, mask=here)
            pltpu.store(acc.at[k, pl.ds(at + CAP, CAP), :], rows, mask=jnp.logical_not(here))
            starts[k] += counts[a, where_am_i[0] * OCC + k]
    saves = [pltpu.make_async_copy(whole.at[k], block.at[k], sems.at[k]) for k in range(OCC)]
    for k in range(OCC):
        whole[k] = acc[k, :NFIT, :].astype(BF16)
        saves[k].start()
        fitted[k, :NFIT] = jnp.dot(metric[k], whole[k], preferred_element_type=F32).astype(BF16)
        fitted[k, NFIT:] = tail[k]
    for save in saves:
        save.wait()


def fit(where_am_i, counts, received, metric, tail):
    smem = pl.BlockSpec(memory_space=pltpu.SMEM)
    vmem = pl.BlockSpec(memory_space=pltpu.VMEM)
    return pl.pallas_call(
        fit_kernel,
        in_specs=[smem, smem, vmem, vmem, vmem],
        out_specs=[vmem, pl.BlockSpec(memory_space=pltpu.HBM)],
        out_shape=[jax.ShapeDtypeStruct((OCC, ROWS, NOSV), BF16), pltpu.HBM((OCC, NFIT, NOSV), BF16)],
        scratch_shapes=[
            pltpu.VMEM((OCC, NFIT + CAP, NOSV), F32),
            pltpu.VMEM((OCC, NFIT, NOSV), BF16),
            pltpu.SemaphoreType.DMA((OCC,)),
        ],
        compiler_params=params(),
        name="fit",
    )(where_am_i, counts, received, metric, tail)


def spread_rows(source, table, starts, at_slot, store):
    sub = lax.broadcasted_iota(I32, (AUXD, 2 * CAP), 0).astype(F32)
    for a in range(NAUX_DEV):
        at = pl.multiple_of(starts[at_slot, a], CAP)
        pick = jnp.where(sub == table[a : a + 1, :], 1.0, 0.0).astype(BF16)
        store(a, jnp.dot(pick, source[pl.ds(at, 2 * CAP), :], preferred_element_type=F32))


def energy_of(tail):
    return tail[1:2, :] + tail[2:3, :] + tail[3:4, :]


def read_starts(sources, starts_v, starts_s, sem):
    for i, source in enumerate(sources):
        starts_v[i : i + 1, :] = source[NFIT + 16 :, :].astype(F32)[0:1, :].astype(I32)
    copy = pltpu.make_async_copy(starts_v, starts_s, sem)
    copy.start()
    copy.wait()


def own_columns(tails):
    rows = [energy_of(t) for t in tails]
    return jnp.concatenate(rows + rows, axis=0).T


def one_round(
    q, slot_of, starts, at_slot, screening, columns, raw_t, spread, ints, amps, energy, density
):
    terms = []
    for l in range(OCC):

        def store(a, value, l=l):
            spread[a * AUXD : (a + 1) * AUXD, l * NOSV : (l + 1) * NOSV] = value.astype(BF16)

        source = slot_of(l)
        tail = source[NFIT:, :].astype(F32)
        terms.append(energy_of(tail[16:, :]))
        spread_rows(source, tail, starts, at_slot + l, store)
    ints[...] = jnp.dot(raw_t[...], spread[...], preferred_element_type=F32)
    for k in range(OCC):
        for l in range(OCC):
            ks = slice(k * NOSV, (k + 1) * NOSV)
            ls = slice(l * NOSV, (l + 1) * NOSV)
            value = ints[ks, ls]
            denominator = columns[:, k : k + 1] + terms[l]
            amp = (screening[k, q, l].astype(F32) * value / denominator).astype(BF16)
            amps[ks, ls] = amp
            part = jnp.sum(amp.astype(F32) * value, axis=0, keepdims=True)
            energy[q, k * OCC + l : k * OCC + l + 1, :] = part

    def add_to(before, after):
        for m in range(NAUX // TILE):
            ms = slice(m * TILE, (m + 1) * TILE)
            value = lax.dot_general(
                spread[ms, :], amps[...], (((1,), (1,)), ((), ())), preferred_element_type=F32
            )
            after[ms, :] = value if before is None else before[ms, :] + value

    density(add_to)


def own_kernel(
    screening, fitted, block_in, raw_out, den, energy,
    block, starts_v, starts_s, spread, ints, amps, sem,
):
    load = pltpu.make_async_copy(block_in, block, sem.at[1])
    load.start()
    read_starts([fitted.at[k] for k in range(OCC)], starts_v, starts_s, sem.at[0])
    load.wait()
    for k in range(OCC):

        def store(a, value, k=k):
            raw_out[k * NOSV : (k + 1) * NOSV, a * AUXD : (a + 1) * AUXD] = value.T.astype(BF16)

        spread_rows(block.at[k], fitted[k, NFIT:, :].astype(F32), starts_s, k, store)
    energy[...] = jnp.zeros(energy.shape, F32)
    columns = own_columns([fitted[k, NFIT + 16 :, :].astype(F32) for k in range(OCC)])

    one_round(
        0, lambda l: fitted.at[l], starts_s, 0, screening, columns, raw_out, spread, ints, amps, energy,
        lambda add_to: add_to(None, den),
    )


def round_scratch():
    return [
        pltpu.VMEM((NAUX, SLAB), BF16),
        pltpu.VMEM((SLAB, SLAB), F32),
        pltpu.VMEM((SLAB, SLAB), BF16),
    ]


def own_round(screening, fitted, block):
    smem = pl.BlockSpec(memory_space=pltpu.SMEM)
    vmem = pl.BlockSpec(memory_space=pltpu.VMEM)
    return pl.pallas_call(
        own_kernel,
        in_specs=[smem, vmem, pl.BlockSpec(memory_space=pltpu.HBM)],
        out_specs=[vmem, vmem, vmem],
        out_shape=[
            jax.ShapeDtypeStruct((SLAB, NAUX), BF16),
            pltpu.VMEM((NAUX, SLAB), F32),
            jax.ShapeDtypeStruct((5, 16, NOSV), F32),
        ],
        scratch_shapes=[
            pltpu.VMEM(block.shape, BF16),
            pltpu.VMEM((8, NOSV), I32),
            pltpu.SMEM((8, NOSV), I32),
        ]
        + round_scratch()
        + [pltpu.SemaphoreType.DMA((2,))],
        compiler_params=params(),
        name="own_round",
    )(screening, fitted, pltpu.with_memory_space_constraint(block, pltpu.HBM))


def phase_kernel(masks, last, pieces, matchings, screening, own_tail, raw_t, den_in, *rest):
    far = rest[: len(pieces)]
    rest = rest[len(pieces) :]
    if last:
        energy, den_out, source, starts_v, starts_s, spread, ints, amps, piece_sems, sem, den, short, sems = rest
    else:
        den, energy, source, starts_v, starts_s, spread, ints, amps, piece_sems, sem = rest

    def wanted(mask):
        found = mask == masks[0]
        for other in masks[1:]:
            found |= mask == other
        return found

    count = wanted(matchings[0, 0]).astype(I32)
    for q in range(1, 4):
        count += wanted(matchings[q, 0]).astype(I32)
    energy[...] = jnp.zeros(energy.shape, F32)

    def fetch(index):
        mask, lo, hi = pieces[index]
        target = source.at[masks.index(mask), pl.ds(lo, hi - lo)]
        return pltpu.make_async_copy(far[index], target, piece_sems.at[index])

    def send(final):
        tiles = NAUX // TILE
        each = NAUX_DEV // tiles
        sends = []
        for m in range(tiles):
            for a in range(m * each, (m + 1) * each):
                for k in range(OCC):
                    part = final[a * AUXD : (a + 1) * AUXD, k * NOSV : (k + 1) * NOSV]
                    short[a, k] = part.astype(BF16)
            owners = pl.ds(m * each, each)
            copy = pltpu.make_async_copy(short.at[owners], den_out.at[owners], sems.at[m])
            copy.start()
            sends.append(copy)
        for copy in sends:
            copy.wait()

    @pl.when(count > 0)
    def _():
        for index in range(len(pieces)):
            fetch(index).start()
        for index in range(len(pieces)):
            fetch(index).wait()
        slots = [source.at[i, l] for i in range(len(masks)) for l in range(OCC)]
        read_starts(slots, starts_v, starts_s, sem.at[0])
        columns = own_columns([own_tail[k, 16:, :].astype(F32) for k in range(OCC)])

        def body(q, done):
            mask = matchings[q, 0]

            def density(add_to):
                @pl.when(done == 0)
                def _():
                    add_to(den_in, den)

                @pl.when(done > 0)
                def _():
                    add_to(den, den)

            @pl.when(wanted(mask))
            def _():
                which = jnp.int32(0)
                for i in range(1, len(masks)):
                    which = jnp.where(mask == masks[i], i, which)
                one_round(
                    q + 1, lambda l: source.at[which, l], starts_s, which * OCC, screening, columns,
                    raw_t, spread, ints, amps, energy, density,
                )

            return done + wanted(mask).astype(I32)

        lax.fori_loop(0, 4, body, jnp.int32(0))
        if last:
            send(den)

    @pl.when(count == 0)
    def _():
        if last:
            send(den_in)
        else:
            den[...] = den_in[...]


def phase(masks, last, pieces, matchings, screening, own_tail, raw_t, den, far):
    smem = pl.BlockSpec(memory_space=pltpu.SMEM)
    vmem = pl.BlockSpec(memory_space=pltpu.VMEM)
    hbm = pl.BlockSpec(memory_space=pl.ANY)
    energy = jax.ShapeDtypeStruct((5, 16, NOSV), F32)
    if last:
        sent = (NAUX_DEV, OCC, AUXD, NOSV)
        out_specs = [vmem, hbm]
        out_shape = [energy, pltpu.HBM(sent, BF16)]
        more = [
            pltpu.VMEM((NAUX, SLAB), F32),
            pltpu.VMEM(sent, BF16),
            pltpu.SemaphoreType.DMA((NAUX // TILE,)),
        ]
        alias = {}
    else:
        out_specs = [vmem, vmem]
        out_shape = [pltpu.VMEM((NAUX, SLAB), F32), energy]
        more = []
        alias = {4: 0}
    rows = -(-len(masks) * OCC // 8) * 8
    return pl.pallas_call(
        functools.partial(phase_kernel, masks, last, pieces),
        in_specs=[smem, smem, vmem, vmem, vmem] + [hbm] * len(far),
        out_specs=out_specs,
        out_shape=out_shape,
        scratch_shapes=[
            pltpu.VMEM((len(masks), OCC, ROWS, NOSV), BF16),
            pltpu.VMEM((rows, NOSV), I32),
            pltpu.SMEM((rows, NOSV), I32),
        ]
        + round_scratch()
        + [pltpu.SemaphoreType.DMA((len(pieces),)), pltpu.SemaphoreType.DMA((1,))]
        + more,
        input_output_aliases=alias,
        compiler_params=params(),
        name="phase_" + "_".join(str(m) for m in masks),
    )(matchings, screening, own_tail, raw_t, pltpu.with_memory_space_constraint(den, pltpu.VMEM), *far)


def widen_kernel(short, wide):
    wide[...] = short[...].astype(F32)


def widen(short):
    blocks = 4
    spec = pl.BlockSpec((short.shape[0] // blocks,) + short.shape[1:], lambda i: (i, 0, 0))
    return pl.pallas_call(
        widen_kernel,
        grid=(blocks,),
        in_specs=[spec],
        out_specs=spec,
        out_shape=jax.ShapeDtypeStruct(short.shape, F32),
        compiler_params=params(),
        name="widen",
    )(short)


def flip(x, mask):
    return lax.ppermute(x, "orb", [(i, i ^ mask) for i in range(lax.axis_size("orb"))])


def per_device(
    raw_rows, fit_metric, domain, counts, orbital_ids, occ_energy, osv_energy, matchings, screening
):
    where_am_i = lax.axis_index("aux").astype(I32).reshape(1)
    group = raw_rows.shape[0]
    counts = counts.T
    packed = pack_rows(where_am_i, domain, counts, raw_rows)
    packed = packed.reshape(NAUX_DEV, OCC, CAP, NOSV)
    received = lax.all_to_all(packed, "aux", split_axis=0, concat_axis=0, tiled=True)
    tail = slot_tables(where_am_i, counts, orbital_ids, occ_energy, domain, osv_energy)
    fitted, block = fit(where_am_i, counts, received, fit_metric, tail)

    near = (flip(fitted, 1), flip(fitted, 2), flip(fitted, 6))
    raw_t, den, energy0 = own_round(screening, fitted, block)
    near, den = lax.optimization_barrier((near, den))
    far1, far2, far6 = near
    middle = (flip(far2, 1), flip(far6, 2), flip(far1, 6))
    common = (matchings, screening, tail, raw_t)
    den, energy1 = phase((1, 2, 6), False, ((1, 0, 4), (2, 0, 4), (6, 0, 4)), *common, den, near)
    middle, den = lax.optimization_barrier((middle, den))
    far3, far4, far7 = middle
    far5 = (flip(far4[0:1], 1), flip(far7[1:2], 2), flip(far3[2:4], 6))
    den, energy2 = phase((3, 4, 7), False, ((3, 0, 4), (4, 0, 4), (7, 0, 4)), *common, den, middle)
    energy3, sent = phase((5,), True, ((5, 0, 1), (5, 1, 2), (5, 2, 4)), *common, den, far5)
    returned = lax.all_to_all(sent, "aux", split_axis=0, concat_axis=0, tiled=True)
    density = widen(returned.reshape(group, AUXD, NOSV))
    total = jnp.sum(energy0 + energy1 + energy2 + energy3, axis=2)
    energies = total.reshape(5, OCC, OCC).transpose(1, 0, 2) * (PAIR_SCALE / (NOSV * NOSV))
    return density, energies


def solution(mesh):
    placed = (
        P("orb", "aux", None),
        P(("orb", "aux"), None, None),
        P("orb", None),
        P("orb", None),
        P(("orb", "aux")),
        P(),
        P(("orb", "aux"), None),
        P(),
        P(("orb", "aux"), None, None),
    )
    return jax.shard_map(
        per_device,
        mesh=mesh,
        in_specs=placed,
        out_specs=(P("orb", "aux", None), P(("orb", "aux"), None, None)),
        check_vma=False,
    )
```

profile of v0, /device:TPU:1, one launch (start us, length us, event | category | flops | bytes accessed | tf_op | source)
XLA Modules:
  0.0 119.7 jit_solution(12659606691162111346)
XLA Ops:
  0.6 0.0 copy-start.1
  0.6 0.0 copy-start.2
  0.7 0.0 copy-start.4
  0.7 0.0 copy-start.5
  0.7 0.0 copy-start.6
  0.7 0.0 copy-start
  0.7 4.2 %pack_rows.1 = bf16[64,64,128]{2,1,0:T(8,128)(2,1)} custom-call(s32[1]{0:T(128)} %bitcast.where_am_i, s32[64,512]{1,0:T(8,128)} %domain_in.1, s32[16,64]{1,0:T(8,128)} %bitcast.6, bf16[64,128,128]{2,1,0:T(8,128)(2,1)} %raw.1), custom_call_target="tpu_custom_call" | custom-call | tf_op jit(solution)/shard_map/pack_rows/pallas_call | solution.py:89
  4.9 9.5 %all-to-all-start = ((bf16[16,4,64,128]{3,2,1,0:T(8,128)(2,1)}), bf16[16,4,64,128]{3,2,1,0:T(8,128)(2,1)S(1)}, u32[]{:S(2)}, u32[]{:S(2)}) async-start(bf16[16,4,64,128]{3,2,1,0:T(8,128)(2,1)} %bitcast.9), calls=%async_computation | async-start | bytes 2097152 | tf_op jit(solution)/shard_map/all_to_all | solution.py:465
  14.4 0.0 copy-done.1
  14.4 0.0 copy-done.2
  14.4 0.0 copy-done.4
  14.4 0.0 copy-done.5
  14.4 0.0 copy-done.6
  14.5 0.0 copy-start.7
  14.5 1.2 slot_tables.1.tail.own_tail
  15.6 0.0 copy-start.3
  15.6 16.0 %all-to-all-done.received = bf16[16,4,64,128]{3,2,1,0:T(8,128)(2,1)S(1)} async-done(((bf16[16,4,64,128]{3,2,1,0:T(8,128)(2,1)}), bf16[16,4,64,128]{3,2,1,0:T(8,128)(2,1)S(1)}, u32[]{:S(2)}, u32[]{:S(2)}) %all-to-all-start) | async-done | bytes 1048608 | tf_op jit(solution)/shard_map/all_to_all | solution.py:465
  31.6 3.3 %fit.1 = (bf16[4,544,128]{2,1,0:T(8,128)(2,1)}, bf16[4,512,128]{2,1,0:T(8,128)(2,1)}) custom-call(s32[1]{0:T(128)} %bitcast.where_am_i, s32[16,64]{1,0:T(8,128)S(1)} %bitcast.8, bf16[16,4,64,128]{3,2,1,0:T(8,128)(2,1)S(1)} %all-to-all-done.received, bf16[4,512,512]{2,1,0:T(8,128)(2,1)S(1)} %copy-done, bf16[4,32,128]{2,1,0:T(8,128)(2,1)S(1)} %slot_tables.1.tail.own_tail), custom_call_target="tpu_custom_call" | custom-call | tf_op jit(solution)/shard_map/fit/pallas_call | solution.py:178
  34.9 2.6 %collective-permute-start.2 = (bf16[4,544,128]{2,1,0:T(8,128)(2,1)}, bf16[4,544,128]{2,1,0:T(8,128)(2,1)S(1)}, u32[]{:S(2)}, u32[]{:S(2)}) collective-permute-start(bf16[4,544,128]{2,1,0:T(8,128)(2,1)} %get-tuple-element.21.fitted), channel_id=1, source_target_pairs={{0,96},{16,112},{32,64},{48,80},{64,32},{80,48},{96,0},{112,16},{1... | collective-permute-start | bytes 1671176 | tf_op jit(solution)/shard_map/ppermute | solution.py:454
  37.5 0.0 collective-permute-start.1
  37.5 0.4 collective-permute-start
  37.9 0.1 copy.21.screening
  38.0 6.1 %own_round.1 = (bf16[512,2048]{1,0:T(8,128)(2,1)S(1)}, f32[2048,512]{1,0:T(8,128)S(1)}, f32[5,16,128]{2,1,0:T(8,128)S(1)}) custom-call(s32[4,5,4]{2,1,0:T(8,128)S(1)} %copy.21.screening, bf16[4,544,128]{2,1,0:T(8,128)(2,1)} %get-tuple-element.21.fitted, bf16[4,512,128]{2,1,0:T(8,128)(2,1)} %get-tuple-element.22.block_in), custom_call_target="tpu_custom_call" | custom-call | tf_op jit(solution)/shard_map/own_round/pallas_call | solution.py:288
  44.2 5.5 %collective-permute-done.2.rest_2_ = bf16[4,544,128]{2,1,0:T(8,128)(2,1)S(1)} collective-permute-done((bf16[4,544,128]{2,1,0:T(8,128)(2,1)}, bf16[4,544,128]{2,1,0:T(8,128)(2,1)S(1)}, u32[]{:S(2)}, u32[]{:S(2)}) %collective-permute-start.2) | collective-permute-done | bytes 557088 | tf_op jit(solution)/shard_map/ppermute | solution.py:454
  49.7 1.0 collective-permute-done.1.rest_1_
  50.6 0.0 collective-permute-done.rest_0_
  50.6 0.4 collective-permute-start.3
  51.1 1.2 collective-permute-start.4
  52.2 0.3 collective-permute-start.5
  52.6 0.0 copy-done.3
  52.6 5.5 %phase_1_2_6.1 = (f32[2048,512]{1,0:T(8,128)S(1)}, f32[5,16,128]{2,1,0:T(8,128)S(1)}) custom-call(s32[4,8]{1,0:T(4,128)S(1)} %copy-done.3, s32[4,5,4]{2,1,0:T(8,128)S(1)} %copy.21.screening, bf16[4,32,128]{2,1,0:T(8,128)(2,1)S(1)} %slot_tables.1.tail.own_tail, bf16[512,2048]{1,0:T(8,128)(2,1)S(1)} %get-tuple-element.23.raw_t, ...), custom_call_target="tpu_custom_call", output_to_operand_aliasing={{0}: (4, {})} | custom-call | tf_op jit(solution)/shard_map/phase_1_2_6/pallas_call | solution.py:416
  58.1 4.6 %collective-permute-done.3.rest_0_ = bf16[4,544,128]{2,1,0:T(8,128)(2,1)S(1)} collective-permute-done((bf16[4,544,128]{2,1,0:T(8,128)(2,1)S(1)}, bf16[4,544,128]{2,1,0:T(8,128)(2,1)S(1)}, u32[]{:S(2)}, u32[]{:S(2)}) %collective-permute-start.3) | collective-permute-done | bytes 557088 | tf_op jit(solution)/shard_map/ppermute | solution.py:454
  62.6 0.1 collective-permute-done.4.rest_1_
  62.8 1.8 %collective-permute-done.5.rest_2_ = bf16[4,544,128]{2,1,0:T(8,128)(2,1)S(1)} collective-permute-done((bf16[4,544,128]{2,1,0:T(8,128)(2,1)S(1)}, bf16[4,544,128]{2,1,0:T(8,128)(2,1)S(1)}, u32[]{:S(2)}, u32[]{:S(2)}) %collective-permute-start.5) | collective-permute-done | bytes 557088 | tf_op jit(solution)/shard_map/ppermute | solution.py:454
  64.6 0.5 collective-permute-start.8
  65.2 1.1 collective-permute-start.6
  66.3 0.1 collective-permute-start.7
  66.4 11.8 %phase_3_4_7.1 = (f32[2048,512]{1,0:T(8,128)S(1)}, f32[5,16,128]{2,1,0:T(8,128)S(1)}) custom-call(s32[4,8]{1,0:T(4,128)S(1)} %copy-done.3, s32[4,5,4]{2,1,0:T(8,128)S(1)} %copy.21.screening, bf16[4,32,128]{2,1,0:T(8,128)(2,1)S(1)} %slot_tables.1.tail.own_tail, bf16[512,2048]{1,0:T(8,128)(2,1)S(1)} %get-tuple-element.23.raw_t, ...), custom_call_target="tpu_custom_call", output_to_operand_aliasing={{0}: (4, {})} | custom-call | tf_op jit(solution)/shard_map/phase_3_4_7/pallas_call | solution.py:416
  78.3 0.0 collective-permute-done.6.rest_0_
  78.3 0.0 collective-permute-done.7.rest_1_
  78.3 0.0 collective-permute-done.8.rest_2_
  78.3 2.5 %phase_5.1 = (f32[5,16,128]{2,1,0:T(8,128)S(1)}, bf16[16,4,128,128]{3,2,1,0:T(8,128)(2,1)}) custom-call(s32[4,8]{1,0:T(4,128)S(1)} %copy-done.3, s32[4,5,4]{2,1,0:T(8,128)S(1)} %copy.21.screening, bf16[4,32,128]{2,1,0:T(8,128)(2,1)S(1)} %slot_tables.1.tail.own_tail, bf16[512,2048]{1,0:T(8,128)(2,1)S(1)} %get-tuple-element.23.raw_t, ...), custom_call_target="tpu_custom_call" | custom-call | tf_op jit(solution)/shard_map/phase_5/pallas_call | solution.py:416
  80.8 8.0 %all-to-all-start.1 = ((bf16[16,4,128,128]{3,2,1,0:T(8,128)(2,1)}), bf16[16,4,128,128]{3,2,1,0:T(8,128)(2,1)S(1)}, u32[]{:S(2)}, u32[]{:S(2)}) async-start(bf16[16,4,128,128]{3,2,1,0:T(8,128)(2,1)} %get-tuple-element.35), calls=%async_computation.1 | async-start | bytes 4194304 | tf_op jit(solution)/shard_map/all_to_all | solution.py:481
  88.8 0.1 add_reduce_fusion
  88.9 0.1 mul.14
  89.0 0.7 copy.22
  89.7 27.6 %all-to-all-done.1 = bf16[16,4,128,128]{3,2,1,0:T(8,128)(2,1)S(1)} async-done(((bf16[16,4,128,128]{3,2,1,0:T(8,128)(2,1)}), bf16[16,4,128,128]{3,2,1,0:T(8,128)(2,1)S(1)}, u32[]{:S(2)}, u32[]{:S(2)}) %all-to-all-start.1) | async-done | bytes 2097184 | tf_op jit(solution)/shard_map/all_to_all | solution.py:481
  117.3 2.4 %widen.1 = f32[64,128,128]{2,1,0:T(8,128)} custom-call(bf16[64,128,128]{2,1,0:T(8,128)(2,1)S(1)} %bitcast.5), custom_call_target="tpu_custom_call" | custom-call | tf_op jit(solution)/shard_map/widen/pallas_call | solution.py:442
  (6 shorter events, 0.1 us)
Async XLA Ops:
  0.6 13.8 %copy-start.1 = (s32[64,512]{1,0:T(8,128)S(1)}, s32[64,512]{1,0:T(8,128)}, u32[]{:S(2)}) copy-start(s32[64,512]{1,0:T(8,128)} %domain_in.1) | copy-start | bytes 393220
  0.6 13.8 %copy-start.2 = (s32[64,16]{0,1:T(8,128)S(1)}, s32[64,16]{0,1:T(8,128)}, u32[]{:S(2)}) copy-start(s32[64,16]{0,1:T(8,128)} %param.12) | copy-start | bytes 12292
  0.7 13.8 %copy-start.4 = (f32[512]{0:T(512)S(1)}, f32[512]{0:T(512)}, u32[]{:S(2)}) copy-start(f32[512]{0:T(512)} %occ.1) | copy-start | bytes 6148
  0.7 13.8 %copy-start.5 = (bf16[4,128]{1,0:T(4,128)(2,1)S(1)}, bf16[4,128]{1,0:T(4,128)(2,1)}, u32[]{:S(2)}) copy-start(bf16[4,128]{1,0:T(4,128)(2,1)} %osv.1) | copy-start | bytes 3076
  0.7 13.8 %copy-start.6 = (s32[4]{0:T(128)S(1)}, s32[4]{0:T(128)}, u32[]{:S(2)}) copy-start(s32[4]{0:T(128)} %ids.1) | copy-start | bytes 52
  0.7 30.9 %copy-start = (bf16[4,512,512]{2,1,0:T(8,128)(2,1)S(1)}, bf16[4,512,512]{2,1,0:T(8,128)(2,1)}, u32[]{:S(2)}) copy-start(bf16[4,512,512]{2,1,0:T(8,128)(2,1)} %metric.1) | copy-start | bytes 6291460
  4.9 26.7 %all-to-all-start = ((bf16[16,4,64,128]{3,2,1,0:T(8,128)(2,1)}), bf16[16,4,64,128]{3,2,1,0:T(8,128)(2,1)S(1)}, u32[]{:S(2)}, u32[]{:S(2)}) async-start(bf16[16,4,64,128]{3,2,1,0:T(8,128)(2,1)} %bitcast.9), calls=%async_computation | async-start | bytes 2097152 | tf_op jit(solution)/shard_map/all_to_all | solution.py:465
  14.5 23.5 %copy-start.7 = (s32[4,5,4]{1,2,0:T(4,128)S(1)}, s32[4,5,4]{1,2,0:T(4,128)}, u32[]{:S(2)}) copy-start(s32[4,5,4]{1,2,0:T(4,128)} %param.17) | copy-start | bytes 964
  15.6 36.9 %copy-start.3 = (s32[4,8]{1,0:T(4,128)S(1)}, s32[4,8]{1,0:T(4,128)}, u32[]{:S(2)}) copy-start(s32[4,8]{1,0:T(4,128)} %matchings.5) | copy-start | bytes 388
  34.9 14.7 %collective-permute-start.2 = (bf16[4,544,128]{2,1,0:T(8,128)(2,1)}, bf16[4,544,128]{2,1,0:T(8,128)(2,1)S(1)}, u32[]{:S(2)}, u32[]{:S(2)}) collective-permute-start(bf16[4,544,128]{2,1,0:T(8,128)(2,1)} %get-tuple-element.21.fitted), channel_id=1, source_target_pairs={{0,96},{16,112},{32,64},{48,80},{64,32},{80,48},{96,0},{112,16},{1... | collective-permute-start | bytes 1671176 | tf_op jit(solution)/shard_map/ppermute | solution.py:454
  37.5 13.1 %collective-permute-start.1 = (bf16[4,544,128]{2,1,0:T(8,128)(2,1)}, bf16[4,544,128]{2,1,0:T(8,128)(2,1)S(1)}, u32[]{:S(2)}, u32[]{:S(2)}) collective-permute-start(bf16[4,544,128]{2,1,0:T(8,128)(2,1)} %get-tuple-element.21.fitted), channel_id=1, source_target_pairs={{0,32},{16,48},{32,0},{48,16},{64,96},{80,112},{96,64},{112,80},{1... | collective-permute-start | bytes 1671176 | tf_op jit(solution)/shard_map/ppermute | solution.py:454
  37.5 13.1 %collective-permute-start = (bf16[4,544,128]{2,1,0:T(8,128)(2,1)}, bf16[4,544,128]{2,1,0:T(8,128)(2,1)S(1)}, u32[]{:S(2)}, u32[]{:S(2)}) collective-permute-start(bf16[4,544,128]{2,1,0:T(8,128)(2,1)} %get-tuple-element.21.fitted), channel_id=1, source_target_pairs={{0,16},{16,0},{32,48},{48,32},{64,80},{80,64},{96,112},{112,96},{1... | collective-permute-start | bytes 1671176 | tf_op jit(solution)/shard_map/ppermute | solution.py:454
  50.6 12.0 %collective-permute-start.3 = (bf16[4,544,128]{2,1,0:T(8,128)(2,1)S(1)}, bf16[4,544,128]{2,1,0:T(8,128)(2,1)S(1)}, u32[]{:S(2)}, u32[]{:S(2)}) collective-permute-start(bf16[4,544,128]{2,1,0:T(8,128)(2,1)S(1)} %collective-permute-done.1.rest_1_), channel_id=1, source_target_pairs={{0,16},{16,0},{32,48},{48,32},{64,80},{80,64},{96,112},{112,96},{1... | collective-permute-start | bytes 1671176 | tf_op jit(solution)/shard_map/ppermute | solution.py:454
  51.1 11.7 %collective-permute-start.4 = (bf16[4,544,128]{2,1,0:T(8,128)(2,1)S(1)}, bf16[4,544,128]{2,1,0:T(8,128)(2,1)S(1)}, u32[]{:S(2)}, u32[]{:S(2)}) collective-permute-start(bf16[4,544,128]{2,1,0:T(8,128)(2,1)S(1)} %collective-permute-done.2.rest_2_), channel_id=1, source_target_pairs={{0,32},{16,48},{32,0},{48,16},{64,96},{80,112},{96,64},{112,80},{1... | collective-permute-start | bytes 1671176 | tf_op jit(solution)/shard_map/ppermute | solution.py:454
  52.2 12.4 %collective-permute-start.5 = (bf16[4,544,128]{2,1,0:T(8,128)(2,1)S(1)}, bf16[4,544,128]{2,1,0:T(8,128)(2,1)S(1)}, u32[]{:S(2)}, u32[]{:S(2)}) collective-permute-start(bf16[4,544,128]{2,1,0:T(8,128)(2,1)S(1)} %collective-permute-done.rest_0_), channel_id=1, source_target_pairs={{0,96},{16,112},{32,64},{48,80},{64,32},{80,48},{96,0},{112,16},{1... | collective-permute-start | bytes 1671176 | tf_op jit(solution)/shard_map/ppermute | solution.py:454
  64.6 13.7 %collective-permute-start.8 = (bf16[2,544,128]{2,1,0:T(8,128)(2,1)S(1)}, bf16[2,544,128]{2,1,0:T(8,128)(2,1)S(1)}, u32[]{:S(2)}, u32[]{:S(2)}) collective-permute-start(bf16[2,544,128]{2,1,0:T(8,128)(2,1)S(1)} %slice.11), channel_id=1, source_target_pairs={{0,96},{16,112},{32,64},{48,80},{64,32},{80,48},{96,0},{112,16},{1... | collective-permute-start | bytes 835592 | tf_op jit(solution)/shard_map/ppermute | solution.py:454
  65.2 13.1 %collective-permute-start.6 = (bf16[1,544,128]{2,1,0:T(8,128)(2,1)S(1)}, bf16[1,544,128]{2,1,0:T(8,128)(2,1)S(1)}, u32[]{:S(2)}, u32[]{:S(2)}) collective-permute-start(bf16[1,544,128]{2,1,0:T(8,128)(2,1)S(1)} %slice.9), channel_id=1, source_target_pairs={{0,16},{16,0},{32,48},{48,32},{64,80},{80,64},{96,112},{112,96},{1... | collective-permute-start | bytes 417800 | tf_op jit(solution)/shard_map/ppermute | solution.py:454
  66.3 12.0 %collective-permute-start.7 = (bf16[1,544,128]{2,1,0:T(8,128)(2,1)S(1)}, bf16[1,544,128]{2,1,0:T(8,128)(2,1)S(1)}, u32[]{:S(2)}, u32[]{:S(2)}) collective-permute-start(bf16[1,544,128]{2,1,0:T(8,128)(2,1)S(1)} %slice.10), channel_id=1, source_target_pairs={{0,32},{16,48},{32,0},{48,16},{64,96},{80,112},{96,64},{112,80},{1... | collective-permute-start | bytes 417800 | tf_op jit(solution)/shard_map/ppermute | solution.py:454
  80.8 36.5 %all-to-all-start.1 = ((bf16[16,4,128,128]{3,2,1,0:T(8,128)(2,1)}), bf16[16,4,128,128]{3,2,1,0:T(8,128)(2,1)S(1)}, u32[]{:S(2)}, u32[]{:S(2)}) async-start(bf16[16,4,128,128]{3,2,1,0:T(8,128)(2,1)} %get-tuple-element.35), calls=%async_computation.1 | async-start | bytes 4194304 | tf_op jit(solution)/shard_map/all_to_all | solution.py:481
where the time goes:
time: 118 us; the launch traced here: 120 us
  waiting for transfers between devices  56.6 us (48%)
  Pallas kernels  37 us (31%)
  starting transfers between devices  24.2 us (21%)
    all_to_all x1, waiting for transfers between devices, per_device(): lax.all_to_all(sent, 'aux', split_axis=0, concat_axis=0, tiled=True)  27.6 us
    pallas_call x3, Pallas kernels, phase(): pl.pallas_call(functools.partial(phase_kernel, masks, last, pieces), in_s...  19.8 us
    all_to_all x1, waiting for transfers between devices, per_device(): lax.all_to_all(packed, 'aux', split_axis=0, concat_axis=0, tiled=True)  16 us
    ppermute x9, waiting for transfers between devices, flip(): lax.ppermute(x, 'orb', [(i, i ^ mask) for i in range(lax.axis_size('orb'))])  13 us
    all_to_all x1, starting transfers between devices, per_device(): lax.all_to_all(packed, 'aux', split_axis=0, concat_axis=0, tiled=True)  9.47 us
    all_to_all x1, starting transfers between devices, per_device(): lax.all_to_all(sent, 'aux', split_axis=0, concat_axis=0, tiled=True)  8 us
    ppermute x9, starting transfers between devices, flip(): lax.ppermute(x, 'orb', [(i, i ^ mask) for i in range(lax.axis_size('orb'))])  6.7 us
    pallas_call x1, Pallas kernels, own_round(): pl.pallas_call(own_kernel, in_specs=[smem, vmem, pl.BlockSpec(memory_spac...  6.1 us
  transfers between devices with their start and end apart: 11, of which 7 were waited for; matrix products, arithmetic and copies ran while one was open for 1% of the time, Pallas kernels for 21%

commit v1 on v0

--- a/solution.py
+++ b/solution.py
@@ -19,10 +19,11 @@
 NAUX = AUXD * NAUX_DEV
 CAP = 64
 CHUNKS = NFIT // CAP
-TAIL = 32
+TAIL = 16
 ROWS = NFIT + TAIL
 TILE = 512
 PARTS = 4
+WIDEN_PARTS = 8
 SLAB = OCC * NOSV
 VMEM_LIMIT = 28 * 1024 * 1024
 
@@ -117,7 +118,8 @@
             if i < 3:
                 windows[2 * i + 1 : 2 * i + 2, :] = row[:, i * NOSV + CAP : (i + 1) * NOSV + CAP]
         table[...] = jnp.zeros(table.shape, F32)
-        starts = jnp.zeros((1, NOSV), I32)
+        firsts = jnp.zeros((1, NOSV), I32)
+        behind = jnp.zeros((1, NOSV), I32)
         start = jnp.int32(0)
         for a in range(NAUX_DEV):
             end = start + counts[a, me * OCC + k]
@@ -126,13 +128,18 @@
             entry = windows[pl.ds(chunk, 1), :]
             entry = jnp.where((lane >= start - at) & (lane < end - at), entry, -1)
             table[a : a + 1, :] = entry.astype(F32)
-            starts = jnp.where(lane == a, at, starts)
+            firsts = jnp.where(lane == a, at, firsts)
+            behind = jnp.where(lane == a, start - at, behind)
             start = end
-        table[16:17, :] = starts.astype(F32)
+        wide = jnp.maximum(table[...], pltpu.roll(table[...], CAP, 1))
+        table[0:8, :] = jnp.where(lane < CAP, wide[0:8], wide[8:16])
+        table[8:16, :] = jnp.zeros((8, NOSV), F32)
+        table[8:9, :] = firsts.astype(F32)
+        table[9:10, :] = behind.astype(F32)
         term = energies[k : k + 1, :] - occ[ids[k]]
         for i in range(3):
             rounded = term.astype(BF16).astype(F32)
-            table[17 + i : 18 + i, :] = rounded
+            table[10 + i : 11 + i, :] = rounded
             term = term - rounded
         out[k] = table[...].astype(BF16)
 
@@ -190,21 +197,31 @@
     )(where_am_i, counts, received, metric, tail)
 
 
-def spread_rows(source, table, starts, at_slot, store):
+def spread_rows(source, tail, starts, at_slot, slots, store):
     sub = lax.broadcasted_iota(I32, (AUXD, 2 * CAP), 0).astype(F32)
+    lane = lax.broadcasted_iota(I32, (1, 2 * CAP), 1)
+    table = tail[0:8, :]
+    turned = pltpu.roll(table, CAP, 1)
+    lower = lax.broadcasted_iota(I32, (8, 2 * CAP), 1) < CAP
+    tables = (jnp.where(lower, table, turned), jnp.where(lower, turned, table))
     for a in range(NAUX_DEV):
         at = pl.multiple_of(starts[at_slot, a], CAP)
-        pick = jnp.where(sub == table[a : a + 1, :], 1.0, 0.0).astype(BF16)
+        behind = starts[slots + at_slot, a]
+        row = tables[a // 8][a % 8 : a % 8 + 1, :]
+        row = jnp.where((lane >= behind) & (lane < behind + CAP), row, -1.0)
+        pick = jnp.where(sub == row, 1.0, 0.0).astype(BF16)
         store(a, jnp.dot(pick, source[pl.ds(at, 2 * CAP), :], preferred_element_type=F32))
 
 
 def energy_of(tail):
-    return tail[1:2, :] + tail[2:3, :] + tail[3:4, :]
+    return tail[10:11, :] + tail[11:12, :] + tail[12:13, :]
 
 
 def read_starts(sources, starts_v, starts_s, sem):
     for i, source in enumerate(sources):
-        starts_v[i : i + 1, :] = source[NFIT + 16 :, :].astype(F32)[0:1, :].astype(I32)
+        tail = source[NFIT:, :].astype(F32)
+        starts_v[i : i + 1, :] = tail[8:9, :].astype(I32)
+        starts_v[len(sources) + i : len(sources) + i + 1, :] = tail[9:10, :].astype(I32)
     copy = pltpu.make_async_copy(starts_v, starts_s, sem)
     copy.start()
     copy.wait()
@@ -216,7 +233,7 @@
 
 
 def one_round(
-    q, slot_of, starts, at_slot, screening, columns, raw_t, spread, ints, amps, energy, density
+    q, slot_of, starts, at_slot, slots, screening, columns, raw_t, spread, ints, amps, energy, density
 ):
     terms = []
     for l in range(OCC):
@@ -226,8 +243,8 @@
 
         source = slot_of(l)
         tail = source[NFIT:, :].astype(F32)
-        terms.append(energy_of(tail[16:, :]))
-        spread_rows(source, tail, starts, at_slot + l, store)
+        terms.append(energy_of(tail))
+        spread_rows(source, tail, starts, at_slot + l, slots, store)
     ints[...] = jnp.dot(raw_t[...], spread[...], preferred_element_type=F32)
     for k in range(OCC):
         for l in range(OCC):
@@ -264,12 +281,12 @@
         def store(a, value, k=k):
             raw_out[k * NOSV : (k + 1) * NOSV, a * AUXD : (a + 1) * AUXD] = value.T.astype(BF16)
 
-        spread_rows(block.at[k], fitted[k, NFIT:, :].astype(F32), starts_s, k, store)
+        spread_rows(block.at[k], fitted[k, NFIT:, :].astype(F32), starts_s, k, OCC, store)
     energy[...] = jnp.zeros(energy.shape, F32)
-    columns = own_columns([fitted[k, NFIT + 16 :, :].astype(F32) for k in range(OCC)])
+    columns = own_columns([fitted[k, NFIT:, :].astype(F32) for k in range(OCC)])
 
     one_round(
-        0, lambda l: fitted.at[l], starts_s, 0, screening, columns, raw_out, spread, ints, amps, energy,
+        0, lambda l: fitted.at[l], starts_s, 0, OCC, screening, columns, raw_out, spread, ints, amps, energy,
         lambda add_to: add_to(None, den),
     )
 
@@ -354,7 +371,7 @@
             fetch(index).wait()
         slots = [source.at[i, l] for i in range(len(masks)) for l in range(OCC)]
         read_starts(slots, starts_v, starts_s, sem.at[0])
-        columns = own_columns([own_tail[k, 16:, :].astype(F32) for k in range(OCC)])
+        columns = own_columns([own_tail[k].astype(F32) for k in range(OCC)])
 
         def body(q, done):
             mask = matchings[q, 0]
@@ -374,7 +391,7 @@
                 for i in range(1, len(masks)):
                     which = jnp.where(mask == masks[i], i, which)
                 one_round(
-                    q + 1, lambda l: source.at[which, l], starts_s, which * OCC, screening, columns,
+                    q + 1, lambda l: source.at[which, l], starts_s, which * OCC, len(masks) * OCC, screening, columns,
                     raw_t, spread, ints, amps, energy, density,
                 )
 
@@ -412,7 +429,7 @@
         out_shape = [pltpu.VMEM((NAUX, SLAB), F32), energy]
         more = []
         alias = {4: 0}
-    rows = -(-len(masks) * OCC // 8) * 8
+    rows = 2 * len(masks) * OCC
     return pl.pallas_call(
         functools.partial(phase_kernel, masks, last, pieces),
         in_specs=[smem, smem, vmem, vmem, vmem] + [hbm] * len(far),
@@ -432,19 +449,26 @@
     )(matchings, screening, own_tail, raw_t, pltpu.with_memory_space_constraint(den, pltpu.VMEM), *far)
 
 
-def widen_kernel(short, wide):
-    wide[...] = short[...].astype(F32)
+def widen_kernel(short, out, wide, sems):
+    part = short.shape[0] // WIDEN_PARTS
+    saves = []
+    for i in range(WIDEN_PARTS):
+        span = pl.ds(i * part, part)
+        wide[span] = short[span].astype(F32)
+        save = pltpu.make_async_copy(wide.at[span], out.at[span], sems.at[i])
+        save.start()
+        saves.append(save)
+    for save in saves:
+        save.wait()
 
 
 def widen(short):
-    blocks = 4
-    spec = pl.BlockSpec((short.shape[0] // blocks,) + short.shape[1:], lambda i: (i, 0, 0))
     return pl.pallas_call(
         widen_kernel,
-        grid=(blocks,),
-        in_specs=[spec],
-        out_specs=spec,
-        out_shape=jax.ShapeDtypeStruct(short.shape, F32),
+        in_specs=[pl.BlockSpec(memory_space=pltpu.VMEM)],
+        out_specs=pl.BlockSpec(memory_space=pltpu.HBM),
+        out_shape=pltpu.HBM(short.shape, F32),
+        scratch_shapes=[pltpu.VMEM(short.shape, F32), pltpu.SemaphoreType.DMA((WIDEN_PARTS,))],
         compiler_params=params(),
         name="widen",
     )(short)

time: 118 us -> 118 us (level); the launches traced: 120 us -> 118 us
  waiting for transfers between devices: 56.6 us -> 52.1 us
  starting transfers between devices: 24.2 us -> 26.4 us
    ppermute x9, waiting for transfers between devices: 13 us -> 8.54 us  [flip(): lax.ppermute(x, 'orb', [(i, i ^ mask) for i in range(lax.axis_size('orb'))])]
    ppermute x9, starting transfers between devices: 6.7 us -> 8.47 us  [flip(): lax.ppermute(x, 'orb', [(i, i ^ mask) for i in range(lax.axis_size('orb'))])]
  transfers between devices with their start and end apart: 11 -> 11, of which waited for: 7 -> 6; matrix products, arithmetic and copies ran while one was open for 1% -> 1% of each run, Pallas kernels for 21% -> 18%
where the time goes in v1:
time: 118 us
  waiting for transfers between devices  52.1 us (44%)
  Pallas kernels  37.6 us (32%)
  starting transfers between devices  26.4 us (22%)
    all_to_all x1, waiting for transfers between devices, per_device(): lax.all_to_all(sent, 'aux', split_axis=0, concat_axis=0, tiled=True)  27.7 us
    pallas_call x3, Pallas kernels, phase(): pl.pallas_call(functools.partial(phase_kernel, masks, last, pieces), in_s...  20.6 us
    all_to_all x1, waiting for transfers between devices, per_device(): lax.all_to_all(packed, 'aux', split_axis=0, concat_axis=0, tiled=True)  15.9 us
    all_to_all x1, starting transfers between devices, per_device(): lax.all_to_all(packed, 'aux', split_axis=0, concat_axis=0, tiled=True)  9.47 us
    ppermute x9, waiting for transfers between devices, flip(): lax.ppermute(x, 'orb', [(i, i ^ mask) for i in range(lax.axis_size('orb'))])  8.54 us
    ppermute x9, starting transfers between devices, flip(): lax.ppermute(x, 'orb', [(i, i ^ mask) for i in range(lax.axis_size('orb'))])  8.47 us
    all_to_all x1, starting transfers between devices, per_device(): lax.all_to_all(sent, 'aux', split_axis=0, concat_axis=0, tiled=True)  8.44 us
    pallas_call x1, Pallas kernels, own_round(): pl.pallas_call(own_kernel, in_specs=[smem, vmem, pl.BlockSpec(memory_spac...  6.12 us
  transfers between devices with their start and end apart: 11, of which 6 were waited for; matrix products, arithmetic and copies ran while one was open for 1% of the time, Pallas kernels for 18%

profile of v1, /device:TPU:1, one launch (start us, length us, event | category | flops | bytes accessed | tf_op | source)
XLA Modules:
  0.0 118.2 jit_solution(4673000684066371235)
XLA Ops:
  0.6 0.0 copy-start.1
  0.6 0.0 copy-start.2
  0.7 0.0 copy-start.4
  0.7 0.0 copy-start.5
  0.7 0.0 copy-start.6
  0.7 0.0 copy-start
  0.7 4.2 %pack_rows.1 = bf16[64,64,128]{2,1,0:T(8,128)(2,1)} custom-call(s32[1]{0:T(128)} %bitcast.where_am_i, s32[64,512]{1,0:T(8,128)} %domain_in.1, s32[16,64]{1,0:T(8,128)} %bitcast.6, bf16[64,128,128]{2,1,0:T(8,128)(2,1)} %raw.1), custom_call_target="tpu_custom_call" | custom-call | tf_op jit(solution)/shard_map/pack_rows/pallas_call | solution.py:90
  4.9 9.5 %all-to-all-start = ((bf16[16,4,64,128]{3,2,1,0:T(8,128)(2,1)}), bf16[16,4,64,128]{3,2,1,0:T(8,128)(2,1)S(1)}, u32[]{:S(2)}, u32[]{:S(2)}) async-start(bf16[16,4,64,128]{3,2,1,0:T(8,128)(2,1)} %bitcast.9), calls=%async_computation | async-start | bytes 2097152 | tf_op jit(solution)/shard_map/all_to_all | solution.py:489
  14.4 0.0 copy-done.1
  14.4 0.0 copy-done.2
  14.4 0.0 copy-done.4
  14.4 0.0 copy-done.5
  14.4 0.0 copy-done.6
  14.5 0.0 copy-start.7
  14.5 1.3 %slot_tables.1.tail.own_tail = bf16[4,16,128]{2,1,0:T(8,128)(2,1)S(1)} custom-call(s32[1]{0:T(128)} %bitcast.where_am_i, s32[16,64]{1,0:T(8,128)S(1)} %bitcast.7, s32[4]{0:T(128)S(1)} %copy-done.6, f32[512]{0:T(512)S(1)} %copy-done.4, s32[64,512]{1,0:T(8,128)S(1)} %copy-done.1, bf16[4,128]{1,0:T(4,128)(2,1)S(1)} %copy-done.5), custom_call_target="tpu_custom_call" | custom-call | tf_op jit(solution)/shard_map/slot_tables/pallas_call | solution.py:150
  15.7 15.9 %all-to-all-done.received = bf16[16,4,64,128]{3,2,1,0:T(8,128)(2,1)S(1)} async-done(((bf16[16,4,64,128]{3,2,1,0:T(8,128)(2,1)}), bf16[16,4,64,128]{3,2,1,0:T(8,128)(2,1)S(1)}, u32[]{:S(2)}, u32[]{:S(2)}) %all-to-all-start) | async-done | bytes 1048608 | tf_op jit(solution)/shard_map/all_to_all | solution.py:489
  31.6 0.0 copy-done
  31.6 3.3 %fit.1 = (bf16[4,528,128]{2,1,0:T(8,128)(2,1)}, bf16[4,512,128]{2,1,0:T(8,128)(2,1)}) custom-call(s32[1]{0:T(128)} %bitcast.where_am_i, s32[16,64]{1,0:T(8,128)S(1)} %bitcast.8, bf16[16,4,64,128]{3,2,1,0:T(8,128)(2,1)S(1)} %all-to-all-done.received, bf16[4,512,512]{2,1,0:T(8,128)(2,1)S(1)} %copy-done, bf16[4,16,128]{2,1,0:T(8,128)(2,1)S(1)} %slot_tables.1.tail.own_tail), custom_call_target="tpu_custom_call" | custom-call | tf_op jit(solution)/shard_map/fit/pallas_call | solution.py:185
  34.9 2.6 %collective-permute-start.2 = (bf16[4,528,128]{2,1,0:T(8,128)(2,1)}, bf16[4,528,128]{2,1,0:T(8,128)(2,1)S(1)}, u32[]{:S(2)}, u32[]{:S(2)}) collective-permute-start(bf16[4,528,128]{2,1,0:T(8,128)(2,1)} %get-tuple-element.21.fitted), channel_id=1, source_target_pairs={{0,96},{16,112},{32,64},{48,80},{64,32},{80,48},{96,0},{112,16},{1... | collective-permute-start | bytes 1622024 | tf_op jit(solution)/shard_map/ppermute | solution.py:478
  37.5 0.0 collective-permute-start.1
  37.5 0.4 collective-permute-start
  37.9 0.1 copy.21.screening
  38.0 6.1 %own_round.1 = (bf16[512,2048]{1,0:T(8,128)(2,1)S(1)}, f32[2048,512]{1,0:T(8,128)S(1)}, f32[5,16,128]{2,1,0:T(8,128)S(1)}) custom-call(s32[4,5,4]{2,1,0:T(8,128)S(1)} %copy.21.screening, bf16[4,528,128]{2,1,0:T(8,128)(2,1)} %get-tuple-element.21.fitted, bf16[4,512,128]{2,1,0:T(8,128)(2,1)} %get-tuple-element.22.block_in), custom_call_target="tpu_custom_call" | custom-call | tf_op jit(solution)/shard_map/own_round/pallas_call | solution.py:305
  44.2 5.1 %collective-permute-done.2.rest_2_ = bf16[4,528,128]{2,1,0:T(8,128)(2,1)S(1)} collective-permute-done((bf16[4,528,128]{2,1,0:T(8,128)(2,1)}, bf16[4,528,128]{2,1,0:T(8,128)(2,1)S(1)}, u32[]{:S(2)}, u32[]{:S(2)}) %collective-permute-start.2) | collective-permute-done | bytes 540704 | tf_op jit(solution)/shard_map/ppermute | solution.py:478
  49.3 1.0 collective-permute-done.1.rest_1_
  50.3 0.0 collective-permute-done.rest_0_
  50.3 0.4 collective-permute-start.3
  50.7 1.2 %collective-permute-start.4 = (bf16[4,528,128]{2,1,0:T(8,128)(2,1)S(1)}, bf16[4,528,128]{2,1,0:T(8,128)(2,1)S(1)}, u32[]{:S(2)}, u32[]{:S(2)}) collective-permute-start(bf16[4,528,128]{2,1,0:T(8,128)(2,1)S(1)} %collective-permute-done.2.rest_2_), channel_id=1, source_target_pairs={{0,32},{16,48},{32,0},{48,16},{64,96},{80,112},{96,64},{112,80},{1... | collective-permute-start | bytes 1622024 | tf_op jit(solution)/shard_map/ppermute | solution.py:478
  51.9 0.3 collective-permute-start.5
  52.2 0.0 copy-done.3
  52.2 12.2 %phase_1_2_6.1 = (f32[2048,512]{1,0:T(8,128)S(1)}, f32[5,16,128]{2,1,0:T(8,128)S(1)}) custom-call(s32[4,8]{1,0:T(4,128)S(1)} %copy-done.3, s32[4,5,4]{2,1,0:T(8,128)S(1)} %copy.21.screening, bf16[4,16,128]{2,1,0:T(8,128)(2,1)S(1)} %slot_tables.1.tail.own_tail, bf16[512,2048]{1,0:T(8,128)(2,1)S(1)} %get-tuple-element.23.raw_t, ...), custom_call_target="tpu_custom_call", output_to_operand_aliasing={{0}: (4, {})} | custom-call | tf_op jit(solution)/shard_map/phase_1_2_6/pallas_call | solution.py:433
  64.4 0.0 collective-permute-done.3.rest_0_
  64.4 0.0 collective-permute-done.4.rest_1_
  64.4 0.0 collective-permute-done.5.rest_2_
  64.5 2.4 %collective-permute-start.8 = (bf16[2,528,128]{2,1,0:T(8,128)(2,1)S(1)}, bf16[2,528,128]{2,1,0:T(8,128)(2,1)S(1)}, u32[]{:S(2)}, u32[]{:S(2)}) collective-permute-start(bf16[2,528,128]{2,1,0:T(8,128)(2,1)S(1)} %slice.11), channel_id=1, source_target_pairs={{0,96},{16,112},{32,64},{48,80},{64,32},{80,48},{96,0},{112,16},{1... | collective-permute-start | bytes 811016 | tf_op jit(solution)/shard_map/ppermute | solution.py:478
  66.9 1.1 collective-permute-start.6
  68.1 0.0 collective-permute-start.7
  68.1 1.4 %phase_3_4_7.1 = (f32[2048,512]{1,0:T(8,128)S(1)}, f32[5,16,128]{2,1,0:T(8,128)S(1)}) custom-call(s32[4,8]{1,0:T(4,128)S(1)} %copy-done.3, s32[4,5,4]{2,1,0:T(8,128)S(1)} %copy.21.screening, bf16[4,16,128]{2,1,0:T(8,128)(2,1)S(1)} %slot_tables.1.tail.own_tail, bf16[512,2048]{1,0:T(8,128)(2,1)S(1)} %get-tuple-element.23.raw_t, ...), custom_call_target="tpu_custom_call", output_to_operand_aliasing={{0}: (4, {})} | custom-call | tf_op jit(solution)/shard_map/phase_3_4_7/pallas_call | solution.py:433
  69.5 1.4 %collective-permute-done.6.rest_0_ = bf16[1,528,128]{2,1,0:T(8,128)(2,1)S(1)} collective-permute-done((bf16[1,528,128]{2,1,0:T(8,128)(2,1)S(1)}, bf16[1,528,128]{2,1,0:T(8,128)(2,1)S(1)}, u32[]{:S(2)}, u32[]{:S(2)}) %collective-permute-start.6) | collective-permute-done | bytes 135200 | tf_op jit(solution)/shard_map/ppermute | solution.py:478
  70.9 1.1 collective-permute-done.7.rest_1_
  71.9 0.0 collective-permute-done.8.rest_2_
  71.9 6.9 %phase_5.1 = (f32[5,16,128]{2,1,0:T(8,128)S(1)}, bf16[16,4,128,128]{3,2,1,0:T(8,128)(2,1)}) custom-call(s32[4,8]{1,0:T(4,128)S(1)} %copy-done.3, s32[4,5,4]{2,1,0:T(8,128)S(1)} %copy.21.screening, bf16[4,16,128]{2,1,0:T(8,128)(2,1)S(1)} %slot_tables.1.tail.own_tail, bf16[512,2048]{1,0:T(8,128)(2,1)S(1)} %get-tuple-element.23.raw_t, ...), custom_call_target="tpu_custom_call" | custom-call | tf_op jit(solution)/shard_map/phase_5/pallas_call | solution.py:433
  78.9 8.4 %all-to-all-start.1 = ((bf16[16,4,128,128]{3,2,1,0:T(8,128)(2,1)}), bf16[16,4,128,128]{3,2,1,0:T(8,128)(2,1)S(1)}, u32[]{:S(2)}, u32[]{:S(2)}) async-start(bf16[16,4,128,128]{3,2,1,0:T(8,128)(2,1)} %get-tuple-element.35), calls=%async_computation.1 | async-start | bytes 4194304 | tf_op jit(solution)/shard_map/all_to_all | solution.py:505
  87.3 0.1 add_reduce_fusion
  87.4 0.1 mul.14
  87.5 0.7 copy.22
  88.2 27.7 %all-to-all-done.1 = bf16[16,4,128,128]{3,2,1,0:T(8,128)(2,1)S(1)} async-done(((bf16[16,4,128,128]{3,2,1,0:T(8,128)(2,1)}), bf16[16,4,128,128]{3,2,1,0:T(8,128)(2,1)S(1)}, u32[]{:S(2)}, u32[]{:S(2)}) %all-to-all-start.1) | async-done | bytes 2097184 | tf_op jit(solution)/shard_map/all_to_all | solution.py:505
  115.9 2.1 %widen.1 = f32[64,128,128]{2,1,0:T(8,128)} custom-call(bf16[64,128,128]{2,1,0:T(8,128)(2,1)S(1)} %bitcast.5), custom_call_target="tpu_custom_call" | custom-call | tf_op jit(solution)/shard_map/widen/pallas_call | solution.py:466
  (6 shorter events, 0.1 us)
Async XLA Ops:
  0.6 13.8 %copy-start.1 = (s32[64,512]{1,0:T(8,128)S(1)}, s32[64,512]{1,0:T(8,128)}, u32[]{:S(2)}) copy-start(s32[64,512]{1,0:T(8,128)} %domain_in.1) | copy-start | bytes 393220
  0.6 13.8 %copy-start.2 = (s32[64,16]{0,1:T(8,128)S(1)}, s32[64,16]{0,1:T(8,128)}, u32[]{:S(2)}) copy-start(s32[64,16]{0,1:T(8,128)} %param.12) | copy-start | bytes 12292
  0.7 13.8 %copy-start.4 = (f32[512]{0:T(512)S(1)}, f32[512]{0:T(512)}, u32[]{:S(2)}) copy-start(f32[512]{0:T(512)} %occ.1) | copy-start | bytes 6148
  0.7 13.8 %copy-start.5 = (bf16[4,128]{1,0:T(4,128)(2,1)S(1)}, bf16[4,128]{1,0:T(4,128)(2,1)}, u32[]{:S(2)}) copy-start(bf16[4,128]{1,0:T(4,128)(2,1)} %osv.1) | copy-start | bytes 3076
  0.7 13.8 %copy-start.6 = (s32[4]{0:T(128)S(1)}, s32[4]{0:T(128)}, u32[]{:S(2)}) copy-start(s32[4]{0:T(128)} %ids.1) | copy-start | bytes 52
  0.7 30.9 %copy-start = (bf16[4,512,512]{2,1,0:T(8,128)(2,1)S(1)}, bf16[4,512,512]{2,1,0:T(8,128)(2,1)}, u32[]{:S(2)}) copy-start(bf16[4,512,512]{2,1,0:T(8,128)(2,1)} %metric.1) | copy-start | bytes 6291460
  4.9 26.7 %all-to-all-start = ((bf16[16,4,64,128]{3,2,1,0:T(8,128)(2,1)}), bf16[16,4,64,128]{3,2,1,0:T(8,128)(2,1)S(1)}, u32[]{:S(2)}, u32[]{:S(2)}) async-start(bf16[16,4,64,128]{3,2,1,0:T(8,128)(2,1)} %bitcast.9), calls=%async_computation | async-start | bytes 2097152 | tf_op jit(solution)/shard_map/all_to_all | solution.py:489
  14.5 23.5 %copy-start.7 = (s32[4,5,4]{1,2,0:T(4,128)S(1)}, s32[4,5,4]{1,2,0:T(4,128)}, u32[]{:S(2)}) copy-start(s32[4,5,4]{1,2,0:T(4,128)} %param.17) | copy-start | bytes 964
  15.7 36.5 %copy-start.3 = (s32[4,8]{1,0:T(4,128)S(1)}, s32[4,8]{1,0:T(4,128)}, u32[]{:S(2)}) copy-start(s32[4,8]{1,0:T(4,128)} %matchings.5) | copy-start | bytes 388
  34.9 14.4 %collective-permute-start.2 = (bf16[4,528,128]{2,1,0:T(8,128)(2,1)}, bf16[4,528,128]{2,1,0:T(8,128)(2,1)S(1)}, u32[]{:S(2)}, u32[]{:S(2)}) collective-permute-start(bf16[4,528,128]{2,1,0:T(8,128)(2,1)} %get-tuple-element.21.fitted), channel_id=1, source_target_pairs={{0,96},{16,112},{32,64},{48,80},{64,32},{80,48},{96,0},{112,16},{1... | collective-permute-start | bytes 1622024 | tf_op jit(solution)/shard_map/ppermute | solution.py:478
  37.5 12.8 %collective-permute-start.1 = (bf16[4,528,128]{2,1,0:T(8,128)(2,1)}, bf16[4,528,128]{2,1,0:T(8,128)(2,1)S(1)}, u32[]{:S(2)}, u32[]{:S(2)}) collective-permute-start(bf16[4,528,128]{2,1,0:T(8,128)(2,1)} %get-tuple-element.21.fitted), channel_id=1, source_target_pairs={{0,32},{16,48},{32,0},{48,16},{64,96},{80,112},{96,64},{112,80},{1... | collective-permute-start | bytes 1622024 | tf_op jit(solution)/shard_map/ppermute | solution.py:478
  37.5 12.8 %collective-permute-start = (bf16[4,528,128]{2,1,0:T(8,128)(2,1)}, bf16[4,528,128]{2,1,0:T(8,128)(2,1)S(1)}, u32[]{:S(2)}, u32[]{:S(2)}) collective-permute-start(bf16[4,528,128]{2,1,0:T(8,128)(2,1)} %get-tuple-element.21.fitted), channel_id=1, source_target_pairs={{0,16},{16,0},{32,48},{48,32},{64,80},{80,64},{96,112},{112,96},{1... | collective-permute-start | bytes 1622024 | tf_op jit(solution)/shard_map/ppermute | solution.py:478
  50.3 14.1 %collective-permute-start.3 = (bf16[4,528,128]{2,1,0:T(8,128)(2,1)S(1)}, bf16[4,528,128]{2,1,0:T(8,128)(2,1)S(1)}, u32[]{:S(2)}, u32[]{:S(2)}) collective-permute-start(bf16[4,528,128]{2,1,0:T(8,128)(2,1)S(1)} %collective-permute-done.1.rest_1_), channel_id=1, source_target_pairs={{0,16},{16,0},{32,48},{48,32},{64,80},{80,64},{96,112},{112,96},{1... | collective-permute-start | bytes 1622024 | tf_op jit(solution)/shard_map/ppermute | solution.py:478
  50.7 13.7 %collective-permute-start.4 = (bf16[4,528,128]{2,1,0:T(8,128)(2,1)S(1)}, bf16[4,528,128]{2,1,0:T(8,128)(2,1)S(1)}, u32[]{:S(2)}, u32[]{:S(2)}) collective-permute-start(bf16[4,528,128]{2,1,0:T(8,128)(2,1)S(1)} %collective-permute-done.2.rest_2_), channel_id=1, source_target_pairs={{0,32},{16,48},{32,0},{48,16},{64,96},{80,112},{96,64},{112,80},{1... | collective-permute-start | bytes 1622024 | tf_op jit(solution)/shard_map/ppermute | solution.py:478
  51.9 12.6 %collective-permute-start.5 = (bf16[4,528,128]{2,1,0:T(8,128)(2,1)S(1)}, bf16[4,528,128]{2,1,0:T(8,128)(2,1)S(1)}, u32[]{:S(2)}, u32[]{:S(2)}) collective-permute-start(bf16[4,528,128]{2,1,0:T(8,128)(2,1)S(1)} %collective-permute-done.rest_0_), channel_id=1, source_target_pairs={{0,96},{16,112},{32,64},{48,80},{64,32},{80,48},{96,0},{112,16},{1... | collective-permute-start | bytes 1622024 | tf_op jit(solution)/shard_map/ppermute | solution.py:478
  64.5 7.4 %collective-permute-start.8 = (bf16[2,528,128]{2,1,0:T(8,128)(2,1)S(1)}, bf16[2,528,128]{2,1,0:T(8,128)(2,1)S(1)}, u32[]{:S(2)}, u32[]{:S(2)}) collective-permute-start(bf16[2,528,128]{2,1,0:T(8,128)(2,1)S(1)} %slice.11), channel_id=1, source_target_pairs={{0,96},{16,112},{32,64},{48,80},{64,32},{80,48},{96,0},{112,16},{1... | collective-permute-start | bytes 811016 | tf_op jit(solution)/shard_map/ppermute | solution.py:478
  66.9 3.9 %collective-permute-start.6 = (bf16[1,528,128]{2,1,0:T(8,128)(2,1)S(1)}, bf16[1,528,128]{2,1,0:T(8,128)(2,1)S(1)}, u32[]{:S(2)}, u32[]{:S(2)}) collective-permute-start(bf16[1,528,128]{2,1,0:T(8,128)(2,1)S(1)} %slice.9), channel_id=1, source_target_pairs={{0,16},{16,0},{32,48},{48,32},{64,80},{80,64},{96,112},{112,96},{1... | collective-permute-start | bytes 405512 | tf_op jit(solution)/shard_map/ppermute | solution.py:478
  68.1 3.9 %collective-permute-start.7 = (bf16[1,528,128]{2,1,0:T(8,128)(2,1)S(1)}, bf16[1,528,128]{2,1,0:T(8,128)(2,1)S(1)}, u32[]{:S(2)}, u32[]{:S(2)}) collective-permute-start(bf16[1,528,128]{2,1,0:T(8,128)(2,1)S(1)} %slice.10), channel_id=1, source_target_pairs={{0,32},{16,48},{32,0},{48,16},{64,96},{80,112},{96,64},{112,80},{1... | collective-permute-start | bytes 405512 | tf_op jit(solution)/shard_map/ppermute | solution.py:478
  78.9 37.0 %all-to-all-start.1 = ((bf16[16,4,128,128]{3,2,1,0:T(8,128)(2,1)}), bf16[16,4,128,128]{3,2,1,0:T(8,128)(2,1)S(1)}, u32[]{:S(2)}, u32[]{:S(2)}) async-start(bf16[16,4,128,128]{3,2,1,0:T(8,128)(2,1)} %get-tuple-element.35), calls=%async_computation.1 | async-start | bytes 4194304 | tf_op jit(solution)/shard_map/all_to_all | solution.py:505
